TPU v7x, 32 devices: a whole 2x2x4 slice. The times are simulated.
32 devices in a mesh: expert: 8 (over z, y), tensor: 4 (over x, core).
Axes of the slice: x: 2, y: 2, z: 4, core: 2. Of those that a mesh axis runs over, the one named last changes fastest.
Arguments:
- attn_partial: bfloat16 [4, 2048, 7168], P('tensor', 'expert'), may hold values from -4 to 4
- residual: bfloat16 [2048, 7168], P(('expert', 'tensor')), may hold values from -6 to 6
- norm_gain: float32 [7168], replicated, may hold values from 0.25 to 1.75
- channel_order: int32 [7168], replicated, may hold values from 0 to 7167, each once
- rotation: bfloat16 [56, 128, 128], replicated, may hold values from -0.5 to 0.5
- routes: int32 [2048, 8], P(('expert', 'tensor')), may hold values from 0 to 31, all different within a row; in each aligned block of 64 rows (0 to 63, 64 to 127, ...) at most 24 rows name the same one
- slab_block: int32 [32], P(('expert', 'tensor')), may hold values from 0 to 52
Outputs:
- hessian: bfloat16 [32, 7168, 512], P(('expert', 'tensor'))
Inputs may be any that keep to these rules, and one draw needn't show every extreme that they name: `routes`: tokens are numbered in the order of their devices along expert+tensor, 256 // 4 a device. Each token names 8 different experts; every expert is named by some token; the tokens of one device name one expert at most 24 times, and exactly 24 times somewhere.
All inputs are finite; a program needn't handle non-finite values.
Results may differ from a plain program's by a relative error of at most 0.018.
Values may be sent and summed in bfloat16 or wider, within the bound.
A program may use at most 128 MiB of HBM per device.

v0:
```python
import jax
import jax.numpy as jnp
from jax import lax
from jax.sharding import PartitionSpec as P

SLAB = 512


def rotate_rows(rows, channel_order, rotation):
    moved = jnp.take(rows, channel_order, axis=1)
    blocks = moved.reshape(rows.shape[0], rotation.shape[0], rotation.shape[1])
    out = jnp.einsum("rbi,bij->rbj", blocks, rotation, preferred_element_type=jnp.float32)
    return out.reshape(rows.shape[0], -1).astype(jnp.bfloat16)


def on_device(attn_partial, residual, norm_gain, channel_order, rotation, routes, slab_block):
    width = residual.shape[1]
    summed = lax.psum_scatter(
        attn_partial[0].astype(jnp.float32).astype(jnp.bfloat16),
        "tensor",
        scatter_dimension=0,
        tiled=True,
    ).astype(jnp.float32)
    hidden = residual.astype(jnp.float32) + summed
    scale = lax.rsqrt(jnp.mean(hidden * hidden, axis=1, keepdims=True) + 1e-06)
    normed = (hidden * scale * norm_gain[None, :]).astype(jnp.bfloat16)
    payload = rotate_rows(normed, channel_order, rotation)
    count_expert = lax.axis_size("expert")
    count_tensor = lax.axis_size("tensor")
    experts = count_expert * count_tensor
    local_rows = normed.shape[0]
    mean_load = local_rows * routes.shape[1] // experts
    slots = max(2, mean_load + (mean_load + 1) // 2)
    expert_ids = jnp.arange(experts, dtype=jnp.int32)
    chosen = jnp.any(routes[:, :, None] == expert_ids[None, None, :], axis=1)
    ranks = jnp.cumsum(chosen.astype(jnp.int32), axis=0) - 1
    slot_ids = jnp.arange(slots, dtype=jnp.int32)
    select = (chosen[:, :, None] & (ranks[:, :, None] == slot_ids[None, None, :])).astype(
        jnp.bfloat16
    )
    occupancy = jnp.sum(select.astype(jnp.float32), axis=0).astype(jnp.bfloat16)
    outgoing = jnp.einsum(
        "rec,rd->ecd", select, payload, preferred_element_type=jnp.float32
    ).astype(jnp.bfloat16)
    outgoing = outgoing.reshape(count_expert, count_tensor, slots, width)
    occupancy = occupancy.reshape(count_expert, count_tensor, slots)
    arrived, filled = (
        lax.all_to_all(
            lax.all_to_all(outgoing, "expert", split_axis=0, concat_axis=0, tiled=True),
            "tensor",
            split_axis=1,
            concat_axis=1,
            tiled=True,
        ),
        lax.all_to_all(
            lax.all_to_all(occupancy, "expert", split_axis=0, concat_axis=0, tiled=True),
            "tensor",
            split_axis=1,
            concat_axis=1,
            tiled=True,
        ),
    )
    rows = arrived.reshape(-1, width)
    count = jnp.sum(filled.astype(jnp.float32))
    start = slab_block[0] * rotation.shape[1]
    slab = lax.dynamic_slice_in_dim(rows, start, SLAB, 1)
    product = lax.dot_general(
        rows, slab, (((0,), (0,)), ((), ())), preferred_element_type=jnp.float32
    )
    return (product * (2.0 / count)).astype(jnp.bfloat16)[None]


def solution(mesh):
    placed = (
        P("tensor", "expert", None),
        P(("expert", "tensor"), None),
        P(),
        P(),
        P(),
        P(("expert", "tensor"), None),
        P(("expert", "tensor")),
    )
    return jax.shard_map(
        on_device,
        mesh=mesh,
        in_specs=placed,
        out_specs=P(("expert", "tensor"), None, None),
        check_vma=False,
    )
```

profile of v0, /device:TPU:0, one launch (start us, length us, event | category | flops | bytes accessed | tf_op | source)
XLA Modules:
  0.0 500.7 jit_solution(12583463592843173925)
XLA Ops:
  6.6 0.7 reduce-scatter.4.cloned.1.call-update
  7.3 0.1 copy-done.6
  7.7 0.8 fusion.9
  8.5 7.3 %all-to-all-start.2 = ((bf16[8,4,24]{2,1,0:T(4,128)(2,1)}), bf16[8,4,24]{2,1,0:T(4,128)(2,1)S(1)}, u32[]{:S(2)}, u32[]{:S(2)}) async-start(bf16[8,4,24]{2,1,0:T(4,128)(2,1)} %bitcast.8), calls=%async_computation.2 | async-start | bytes 16384 | tf_op jit(solution)/shard_map/all_to_all | solution.py:56
  15.8 38.1 %reduce-scatter.4.cloned.1.call-done = bf16[64,7168]{1,0:T(8,128)(2,1)} async-done(((bf16[256,7168]{1,0:T(8,128)(2,1)}), bf16[64,7168]{1,0:T(8,128)(2,1)}) %reduce-scatter.4.cloned.1.call-update) | async-done | bytes 917520 | tf_op jit(solution)/shard_map/reduce_scatter | solution.py:18
  53.9 1.7 multiply_reduce_fusion
  55.6 1.3 multiply_convert_fusion.1
  56.8 2.6 copy.62
  59.4 26.3 %gather_fusion = bf16[7168,64]{1,0:T(8,128)(2,1)} fusion(bf16[64,7168]{0,1:T(8,128)(2,1)} %copy.62, s32[7168]{0:T(1024)S(1)} %fusion.13), kind=kCustom, calls=%fused_computation | custom fusion | bytes 1863680 | tf_op jit(solution)/shard_map/jit(_take)/gather | solution.py:10
  85.8 1.9 copy.63
  87.7 0.6 fusion.1
  88.3 0.6 copy.64
  88.9 0.4 reshape.57
  89.3 5.6 %convolution_convert_fusion = bf16[32,24,7168]{2,1,0:T(8,128)(2,1)} fusion(bf16[64,7168,1]{1,0,2:T(8,128)(2,1)S(1)} %reshape.57, s32[64,32]{0,1:T(8,128)S(1)} %copy.59, pred[64,32]{0,1:T(8,128)(4,1)S(1)} %fusion.12), kind=kOutput, calls=%fused_computation.2 | convolution fusion | flops 710246400 | bytes 11937792 | tf_op jit(solution)/shard_map/rec,rd->ecd/dot_general | solution.py:42
  94.9 5.5 %all-to-all-start = ((bf16[8,4,24,7168]{3,2,1,0:T(8,128)(2,1)}), bf16[8,4,24,7168]{3,2,1,0:T(8,128)(2,1)}, u32[]{:S(2)}, u32[]{:S(2)}) async-start(bf16[8,4,24,7168]{3,2,1,0:T(8,128)(2,1)} %bitcast.19), calls=%async_computation | async-start | bytes 22020096 | tf_op jit(solution)/shard_map/all_to_all | solution.py:49
  100.4 0.6 copy.67
  101.0 238.6 %all-to-all-done = bf16[8,4,24,7168]{3,2,1,0:T(8,128)(2,1)} async-done(((bf16[8,4,24,7168]{3,2,1,0:T(8,128)(2,1)}), bf16[8,4,24,7168]{3,2,1,0:T(8,128)(2,1)}, u32[]{:S(2)}, u32[]{:S(2)}) %all-to-all-start) | async-done | bytes 11010080 | tf_op jit(solution)/shard_map/all_to_all | solution.py:49
  339.6 3.2 all-to-all-start.3
  342.8 9.6 %copy.65 = bf16[8,4,24,7168]{3,2,0,1:T(8,128)(2,1)} copy(bf16[8,4,24,7168]{3,2,1,0:T(8,128)(2,1)} %all-to-all-done) | data formatting | bytes 22020096 | tf_op jit(solution)/shard_map/all_to_all | solution.py:49
  352.4 6.1 %all-to-all-start.1 = ((bf16[8,4,24,7168]{3,2,0,1:T(8,128)(2,1)}), bf16[8,4,24,7168]{3,2,0,1:T(8,128)(2,1)}, u32[]{:S(2)}, u32[]{:S(2)}) async-start(bf16[8,4,24,7168]{3,2,0,1:T(8,128)(2,1)} %copy.65), calls=%async_computation.1 | async-start | bytes 22020096 | tf_op jit(solution)/shard_map/all_to_all | solution.py:48
  359.2 0.6 convert_reduce_fusion
  360.5 119.3 %all-to-all-done.1 = bf16[8,4,24,7168]{3,2,0,1:T(8,128)(2,1)} async-done(((bf16[8,4,24,7168]{3,2,0,1:T(8,128)(2,1)}), bf16[8,4,24,7168]{3,2,0,1:T(8,128)(2,1)}, u32[]{:S(2)}, u32[]{:S(2)}) %all-to-all-start.1) | async-done | bytes 11010080 | tf_op jit(solution)/shard_map/all_to_all | solution.py:48
  479.8 5.9 %copy.66 = bf16[8,4,24,7168]{3,2,1,0:T(8,128)(2,1)S(1)} copy(bf16[8,4,24,7168]{3,2,0,1:T(8,128)(2,1)} %all-to-all-done.1) | data formatting | bytes 22020096 | tf_op jit(solution)/shard_map/all_to_all | solution.py:48
  485.7 8.2 %fusion = bf16[1,7168,512]{2,1,0:T(8,128)(2,1)} fusion(bf16[768,7168]{1,0:T(8,128)(2,1)S(1)} %bitcast.20, f32[]{:T(128)S(6)} %div.11, s32[]{:T(128)S(6)} %select_n.15), kind=kOutput, calls=%fused_computation.3 | convolution fusion | flops 5644484608 | bytes 19136520 | tf_op jit(solution)/shard_map/dot_general | solution.py:67
  (25 shorter events, 0.3 us)
Async XLA Ops:
  6.5 81.1 %copy-start = (bf16[56,128,128]{2,1,0:T(8,128)(2,1)S(1)}, bf16[56,128,128]{2,1,0:T(8,128)(2,1)}, u32[]{:S(2)}) copy-start(bf16[56,128,128]{2,1,0:T(8,128)(2,1)} %param.11) | copy-start | bytes 5505028
  6.5 47.3 %reduce-scatter.4.cloned.1.call-start = ((), (), s32[]{:S(2)}) async-start(), calls=%async_computation.5 | async-start | bytes 4587520 | tf_op jit(solution)/shard_map/reduce_scatter | solution.py:18
  6.5 0.8 copy-start.6
  6.5 9.2 %copy-start.4 = (s32[7168]{0:T(1024)S(1)}, s32[7168]{0:T(1024)}, u32[]{:S(2)}) copy-start(s32[7168]{0:T(1024)} %param.10) | copy-start | bytes 86020
  6.5 47.3 %copy-start.2 = (bf16[64,7168]{1,0:T(8,128)(2,1)S(1)}, bf16[64,7168]{1,0:T(8,128)(2,1)}, u32[]{:S(2)}) copy-start(bf16[64,7168]{1,0:T(8,128)(2,1)} %param.8) | copy-start | bytes 2752516
  7.4 48.2 %copy-start.5 = (f32[7168]{0:T(1024)S(1)}, f32[7168]{0:T(1024)}, u32[]{:S(2)}) copy-start(f32[7168]{0:T(1024)} %param.9) | copy-start | bytes 86020
  8.5 86.4 %all-to-all-start.2 = ((bf16[8,4,24]{2,1,0:T(4,128)(2,1)}), bf16[8,4,24]{2,1,0:T(4,128)(2,1)S(1)}, u32[]{:S(2)}, u32[]{:S(2)}) async-start(bf16[8,4,24]{2,1,0:T(4,128)(2,1)} %bitcast.8), calls=%async_computation.2 | async-start | bytes 16384 | tf_op jit(solution)/shard_map/all_to_all | solution.py:56
  53.9 1.7 copy-start.3
  94.9 244.7 %all-to-all-start = ((bf16[8,4,24,7168]{3,2,1,0:T(8,128)(2,1)}), bf16[8,4,24,7168]{3,2,1,0:T(8,128)(2,1)}, u32[]{:S(2)}, u32[]{:S(2)}) async-start(bf16[8,4,24,7168]{3,2,1,0:T(8,128)(2,1)} %bitcast.19), calls=%async_computation | async-start | bytes 22020096 | tf_op jit(solution)/shard_map/all_to_all | solution.py:49
  339.6 12.8 %all-to-all-start.3 = ((bf16[8,4,24]{2,0,1:T(8,128)(2,1)}), bf16[8,4,24]{2,0,1:T(8,128)(2,1)S(1)}, u32[]{:S(2)}, u32[]{:S(2)}) async-start(bf16[8,4,24]{2,0,1:T(8,128)(2,1)} %copy.67), calls=%async_computation.3 | async-start | bytes 16384 | tf_op jit(solution)/shard_map/all_to_all | solution.py:55
  352.4 127.3 %all-to-all-start.1 = ((bf16[8,4,24,7168]{3,2,0,1:T(8,128)(2,1)}), bf16[8,4,24,7168]{3,2,0,1:T(8,128)(2,1)}, u32[]{:S(2)}, u32[]{:S(2)}) async-start(bf16[8,4,24,7168]{3,2,0,1:T(8,128)(2,1)} %copy.65), calls=%async_computation.1 | async-start | bytes 22020096 | tf_op jit(solution)/shard_map/all_to_all | solution.py:48
  485.7 8.2 %copy-start.1 = (bf16[56,128,128]{2,1,0:T(8,128)(2,1)S(1)}, bf16[56,128,128]{2,1,0:T(8,128)(2,1)}, u32[]{:S(2)}) copy-start(bf16[56,128,128]{2,1,0:T(8,128)(2,1)} %param.11) | copy-start | bytes 5505028
Sparse Core Ops, SparseCore 0:
  9.9 43.9 reduce-scatter.3
where the time goes:
time: 501 us
  waiting for transfers between devices  397 us (79%)
  local copies, waits for them, and re-layouts  48.1 us (10%)
  starting transfers between devices  22.2 us (4%)
  between operations  14.9 us (3%)
  matrix products  14.4 us (3%)
    all_to_all x1, waiting for transfers between devices, on_device(): lax.all_to_all(outgoing, 'expert', split_axis=0, concat_axis=0, tiled=True)  239 us
    all_to_all x1, waiting for transfers between devices, on_device(): lax.all_to_all(lax.all_to_all(outgoing, 'expert', split_axis=0, concat_ax...  119 us
    reduce_scatter x1, waiting for transfers between devices, on_device(): lax.psum_scatter(attn_partial[0].astype(jnp.float32).astype(jnp.bfloat16)...  38.1 us
    gather x2, local copies, waits for them, and re-layouts, rotate_rows(): moved = jnp.take(rows, channel_order, axis=1)  28.2 us
  transfers between devices with their start and end apart: 5, of which 3 were waited for; matrix products, arithmetic and copies ran while one was open for 11% of the time, Pallas kernels for 0%

commit v1 on v0

--- a/solution.py
+++ b/solution.py
@@ -13,22 +13,11 @@
     return out.reshape(rows.shape[0], -1).astype(jnp.bfloat16)
 
 
-def on_device(attn_partial, residual, norm_gain, channel_order, rotation, routes, slab_block):
-    width = residual.shape[1]
-    summed = lax.psum_scatter(
-        attn_partial[0].astype(jnp.float32).astype(jnp.bfloat16),
-        "tensor",
-        scatter_dimension=0,
-        tiled=True,
-    ).astype(jnp.float32)
-    hidden = residual.astype(jnp.float32) + summed
-    scale = lax.rsqrt(jnp.mean(hidden * hidden, axis=1, keepdims=True) + 1e-06)
-    normed = (hidden * scale * norm_gain[None, :]).astype(jnp.bfloat16)
-    payload = rotate_rows(normed, channel_order, rotation)
+def dispatch_rows(payload, routes):
     count_expert = lax.axis_size("expert")
     count_tensor = lax.axis_size("tensor")
     experts = count_expert * count_tensor
-    local_rows = normed.shape[0]
+    local_rows = payload.shape[0]
     mean_load = local_rows * routes.shape[1] // experts
     slots = max(2, mean_load + (mean_load + 1) // 2)
     expert_ids = jnp.arange(experts, dtype=jnp.int32)
@@ -42,7 +31,7 @@
     outgoing = jnp.einsum(
         "rec,rd->ecd", select, payload, preferred_element_type=jnp.float32
     ).astype(jnp.bfloat16)
-    outgoing = outgoing.reshape(count_expert, count_tensor, slots, width)
+    outgoing = outgoing.reshape(count_expert, count_tensor, slots, payload.shape[1])
     occupancy = occupancy.reshape(count_expert, count_tensor, slots)
     arrived, filled = (
         lax.all_to_all(
@@ -60,10 +49,42 @@
             tiled=True,
         ),
     )
-    rows = arrived.reshape(-1, width)
+    rows = arrived.reshape(-1, payload.shape[1])
     count = jnp.sum(filled.astype(jnp.float32))
+    return rows, count
+
+
+def gather_rows(payload, routes):
+    own = lax.axis_index("expert") * lax.axis_size("tensor") + lax.axis_index("tensor")
+    named = lax.all_gather(routes, ("expert", "tensor"), axis=0, tiled=True)
+    chosen = jnp.any(named == own, axis=1)
+    rows = lax.all_gather(payload, ("expert", "tensor"), axis=0, tiled=True)
+    count = jnp.sum(chosen.astype(jnp.float32))
+    return rows, chosen, count
+
+
+def on_device(attn_partial, residual, norm_gain, channel_order, rotation, routes, slab_block):
+    summed = lax.psum_scatter(
+        attn_partial[0].astype(jnp.float32).astype(jnp.bfloat16),
+        "tensor",
+        scatter_dimension=0,
+        tiled=True,
+    ).astype(jnp.float32)
+    hidden = residual.astype(jnp.float32) + summed
+    scale = lax.rsqrt(jnp.mean(hidden * hidden, axis=1, keepdims=True) + 1e-06)
+    normed = (hidden * scale * norm_gain[None, :]).astype(jnp.bfloat16)
+    payload = rotate_rows(normed, channel_order, rotation)
+    experts = lax.axis_size("expert") * lax.axis_size("tensor")
+    mean_load = residual.shape[0] * routes.shape[1] // experts
+    slots = max(2, mean_load + (mean_load + 1) // 2)
     start = slab_block[0] * rotation.shape[1]
-    slab = lax.dynamic_slice_in_dim(rows, start, SLAB, 1)
+    if residual.shape[0] <= 4 * slots:
+        rows, chosen, count = gather_rows(payload, routes)
+        slab = lax.dynamic_slice_in_dim(rows, start, SLAB, 1)
+        slab = slab * chosen[:, None].astype(slab.dtype)
+    else:
+        rows, count = dispatch_rows(payload, routes)
+        slab = lax.dynamic_slice_in_dim(rows, start, SLAB, 1)
     product = lax.dot_general(
         rows, slab, (((0,), (0,)), ((), ())), preferred_element_type=jnp.float32
     )

time: 501 us -> 295 us (0.59)
  waiting for transfers between devices: 397 us -> 178 us
  blocking collectives: 0 us -> 42.1 us
  starting transfers between devices: 22.2 us -> 0.04 us
  local copies, waits for them, and re-layouts: 48.1 us -> 32.1 us
  matrix products: 14.4 us -> 24.2 us
    all_to_all x4 -> x0, waiting for transfers between devices: 358 us -> none  [the longest x1 239 us: on_device(): lax.all_to_all(outgoing, 'expert', split_axis=0, concat_axis=0, tiled=True)]
    all_gather x0 -> x1, waiting for transfers between devices: none -> 131 us  [gather_rows(): rows = lax.all_gather(payload, ('expert', 'tensor'), axis=0, tiled=True)]
    all_gather x0 -> x1, blocking collectives: none -> 42.1 us  [gather_rows(): named = lax.all_gather(routes, ('expert', 'tensor'), axis=0, tiled=True)]
    all_to_all x4 -> x0, starting transfers between devices: 22.2 us -> none  [the longest x1 7.31 us: on_device(): lax.all_to_all(occupancy, 'expert', split_axis=0, concat_axis=0, tiled=True)]
    all_to_all x3 -> x0, local copies, waits for them, and re-layouts: 16 us -> none  [the longest x1 9.58 us: on_device(): lax.all_to_all(outgoing, 'expert', split_axis=0, concat_axis=0, tiled=True)]
    dot_general x1, matrix products: 8.18 us -> 23.6 us  [on_device(): lax.dot_general(rows, slab, (((0,), (0,)), ((), ())), preferred_element_t...]
    reduce_scatter x1, waiting for transfers between devices: 38.1 us -> 46.4 us  [on_device(): lax.psum_scatter(attn_partial[0].astype(jnp.float32).astype(jnp.bfloat16)...]
    dot_general x1 -> x0, matrix products: 5.62 us -> none  [on_device(): jnp.einsum('rec,rd->ecd', select, payload, preferred_element_type=jnp.flo...]
  transfers between devices with their start and end apart: 5 -> 2, of which waited for: 3 -> 2; matrix products, arithmetic and copies ran while one was open for 11% -> 0% of each run, Pallas kernels for 0% -> 0%
where the time goes in v1:
time: 295 us
  waiting for transfers between devices  178 us (60%)
  blocking collectives  42.1 us (14%)
  local copies, waits for them, and re-layouts  32.1 us (11%)
  matrix products  24.2 us (8%)
  between operations  14.8 us (5%)
  other arithmetic  3.67 us (1%)
    all_gather x1, waiting for transfers between devices, gather_rows(): rows = lax.all_gather(payload, ('expert', 'tensor'), axis=0, tiled=True)  131 us
    reduce_scatter x1, waiting for transfers between devices, on_device(): lax.psum_scatter(attn_partial[0].astype(jnp.float32).astype(jnp.bfloat16)...  46.4 us
    all_gather x1, blocking collectives, gather_rows(): named = lax.all_gather(routes, ('expert', 'tensor'), axis=0, tiled=True)  42.1 us
    gather x2, local copies, waits for them, and re-layouts, rotate_rows(): moved = jnp.take(rows, channel_order, axis=1)  28.2 us
    dot_general x1, matrix products, on_device(): lax.dot_general(rows, slab, (((0,), (0,)), ((), ())), preferred_element_t...  23.6 us
  transfers between devices with their start and end apart: 2, of which 2 were waited for; matrix products, arithmetic and copies ran while one was open for 0% of the time, Pallas kernels for 0%

profile of v1, /device:TPU:0, one launch (start us, length us, event | category | flops | bytes accessed | tf_op | source)
XLA Modules:
  0.0 294.6 jit_solution(9188609054125106272)
XLA Ops:
  6.5 0.0 copy-start
  6.5 0.0 reduce-scatter.4.cloned.1.call-start
  6.5 0.7 reduce-scatter.4.cloned.1.call-update
  7.3 0.0 copy-start.4
  7.3 0.0 all-gather.3.cloned.1.call-start
  7.3 0.1 copy-done.3
  7.5 46.4 %reduce-scatter.4.cloned.1.call-done = bf16[64,7168]{1,0:T(8,128)(2,1)} async-done(((bf16[256,7168]{1,0:T(8,128)(2,1)}), bf16[64,7168]{1,0:T(8,128)(2,1)}) %reduce-scatter.4.cloned.1.call-update) | async-done | bytes 917520 | tf_op jit(solution)/shard_map/reduce_scatter | solution.py:67
  53.9 0.0 copy-done.1
  53.9 1.7 multiply_reduce_fusion
  55.6 1.3 multiply_convert_fusion.1
  56.9 2.6 copy.25
  59.4 26.3 %gather_fusion = bf16[7168,64]{1,0:T(8,128)(2,1)} fusion(bf16[64,7168]{0,1:T(8,128)(2,1)} %copy.25, s32[7168]{0:T(1024)S(1)} %fusion.8), kind=kCustom, calls=%fused_computation | custom fusion | bytes 1863680 | tf_op jit(solution)/shard_map/jit(_take)/gather | solution.py:10
  85.8 1.9 copy.26
  87.7 0.6 fusion.3
  88.3 0.0 copy-start.5
  88.3 1.1 copy.33
  89.4 0.0 all-gather.3.cloned.1.call-update
  90.1 0.0 copy-done.5
  90.1 42.1 %all-gather = s32[32,64,8]{1,2,0:T(8,128)S(1)} all-gather(s32[1,64,8]{1,2,0:T(8,128)S(1)} %bitcast.23), channel_id=1, replica_groups=mesh['expert'=8,'tensor'=4] {'expert','tensor'}, dimensions={0}, use_global_device_ids=true | all-gather | bytes 67584 | tf_op jit(solution)/shard_map/all_gather | solution.py:59
  132.1 0.1 compare_reduce_fusion
  132.2 0.1 reshape.43
  132.3 0.6 convert_reduce_fusion
  133.6 130.6 %all-gather.3.cloned.1.call-done = bf16[2048,7168]{1,0:T(8,128)(2,1)} async-done(((bf16[64,7168]{1,0:T(8,128)(2,1)}), bf16[2048,7168]{1,0:T(8,128)(2,1)}) %all-gather.3.cloned.1.call-update) | async-done | bytes 29360144 | tf_op jit(solution)/shard_map/all_gather | solution.py:61
  264.2 23.6 %fusion = bf16[1,7168,512]{2,1,0:T(8,128)(2,1)} fusion(bf16[2048,7168]{1,0:T(8,128)(2,1)} %all-gather.3.cloned.1.call-done, f32[]{:T(128)S(6)} %div.11, s32[]{:T(128)S(6)} %select_n.15, bf16[2048]{0:T(1024)(128)(2,1)S(1)} %reshape.43), kind=kOutput, calls=%fused_computation.2 | convolution fusion | flops 15043919872 | bytes 38801416 | tf_op jit(solution)/shard_map/dot_general | solution.py:88
  (10 shorter events, 0.0 us)
Async XLA Ops:
  6.5 81.1 %copy-start = (bf16[56,128,128]{2,1,0:T(8,128)(2,1)S(1)}, bf16[56,128,128]{2,1,0:T(8,128)(2,1)}, u32[]{:S(2)}) copy-start(bf16[56,128,128]{2,1,0:T(8,128)(2,1)} %param.11) | copy-start | bytes 5505028
  6.5 47.3 %reduce-scatter.4.cloned.1.call-start = ((), (), s32[]{:S(2)}) async-start(), calls=%async_computation.2 | async-start | bytes 4587520 | tf_op jit(solution)/shard_map/reduce_scatter | solution.py:67
  6.5 0.9 copy-start.3
  6.5 47.3 %copy-start.1 = (bf16[64,7168]{1,0:T(8,128)(2,1)S(1)}, bf16[64,7168]{1,0:T(8,128)(2,1)}, u32[]{:S(2)}) copy-start(bf16[64,7168]{1,0:T(8,128)(2,1)} %param.8) | copy-start | bytes 2752516
  7.3 48.3 %copy-start.4 = (f32[7168]{0:T(1024)S(1)}, f32[7168]{0:T(1024)}, u32[]{:S(2)}) copy-start(f32[7168]{0:T(1024)} %param.9) | copy-start | bytes 86020
  7.3 256.9 %all-gather.3.cloned.1.call-start = ((), (), s32[]{:S(2)}) async-start(), calls=%async_computation.1 | async-start | bytes 30277632 | tf_op jit(solution)/shard_map/all_gather | solution.py:61
  53.9 1.7 copy-start.2
  88.3 1.8 copy-start.5
Sparse Core Ops, SparseCore 0:
  9.9 43.9 reduce-scatter.3
  89.5 174.6 all-gather.2

commit v2 on v1

--- a/solution.py
+++ b/solution.py
@@ -1,6 +1,10 @@
+import functools
+
 import jax
 import jax.numpy as jnp
 from jax import lax
+from jax.experimental import pallas as pl
+from jax.experimental.pallas import tpu as pltpu
 from jax.sharding import PartitionSpec as P
 
 SLAB = 512
@@ -54,13 +58,302 @@
     return rows, count
 
 
-def gather_rows(payload, routes):
-    own = lax.axis_index("expert") * lax.axis_size("tensor") + lax.axis_index("tensor")
-    named = lax.all_gather(routes, ("expert", "tensor"), axis=0, tiled=True)
-    chosen = jnp.any(named == own, axis=1)
-    rows = lax.all_gather(payload, ("expert", "tensor"), axis=0, tiled=True)
-    count = jnp.sum(chosen.astype(jnp.float32))
-    return rows, chosen, count
+def line_order(length):
+    orders = []
+    for at in range(length):
+        near = -1 if 2 * at < length else 1
+        hops = [d for far in range(1, length) for d in (near * far, -near * far)]
+        orders.append([at + d for d in hops if 0 <= at + d < length])
+    return orders
+
+
+def gram_kernel(
+    planes, local, width, columns,
+    bits_ref, own_ref, out_ref,
+    rows, picked, moved, slab, total, staged, own_sem, send_sem, recv_sem, out_sem,
+):
+    expert, tensor = lax.axis_index("expert"), lax.axis_index("tensor")
+    plane, side = lax.div(expert, 2), lax.rem(expert, 2)
+    pair, core = lax.div(tensor, 2), lax.rem(tensor, 2)
+    half = local // 2
+    orders = line_order(planes)
+
+    def table(values):
+        total_of = 0
+        for at, value in enumerate(values):
+            total_of = total_of + value * lax.div(
+                planes - lax.rem(plane + planes - at, planes), planes
+            )
+        return total_of
+
+    def block(z, y, x, c):
+        return (z * 2 + y) * 4 + x * 2 + c
+
+    def device(z, y, x, c):
+        return (z * 2 + y, x * 2 + c)
+
+    def piece(number, h):
+        return rows.at[pl.ds(pl.multiple_of(number * local + h * half, half), half), :]
+
+    sends = []
+
+    def send(number, h, target):
+        copy = pltpu.make_async_remote_copy(
+            src_ref=piece(number, h),
+            dst_ref=piece(number, h),
+            send_sem=send_sem.at[len(sends)],
+            recv_sem=recv_sem.at[number, h],
+            device_id=target,
+            device_id_type=pl.DeviceIdType.MESH,
+        )
+        sends.append(copy)
+        return copy
+
+    def arrive(number, h):
+        pltpu.make_async_remote_copy(
+            src_ref=piece(number, h),
+            dst_ref=piece(number, h),
+            send_sem=send_sem.at[0],
+            recv_sem=recv_sem.at[number, h],
+            device_id=other_core,
+            device_id_type=pl.DeviceIdType.MESH,
+        ).wait_recv()
+
+    other_pair = device(plane, side, 1 - pair, core)
+    other_side = device(plane, 1 - side, pair, core)
+    other_core = device(plane, side, pair, 1 - core)
+    has_above = table([1 if at + 1 < planes else 0 for at in range(planes)])
+    has_below = table([1 if at >= 1 else 0 for at in range(planes)])
+    above = table([min(at + 1, planes - 1) for at in range(planes)])
+    below = table([max(at - 1, 0) for at in range(planes)])
+
+    fetch = pltpu.make_async_copy(
+        own_ref,
+        rows.at[pl.ds(pl.multiple_of(block(plane, side, pair, core) * local, local), local), :],
+        own_sem,
+    )
+    fetch.start()
+
+    barrier = pltpu.get_barrier_semaphore()
+    for peer in (other_pair, other_side, other_core):
+        pl.semaphore_signal(
+            barrier, inc=1, device_id=peer, device_id_type=pl.DeviceIdType.MESH
+        )
+
+    @pl.when(has_above == 1)
+    def _():
+        pl.semaphore_signal(
+            barrier, inc=1, device_id=device(above, side, pair, core),
+            device_id_type=pl.DeviceIdType.MESH,
+        )
+
+    @pl.when(has_below == 1)
+    def _():
+        pl.semaphore_signal(
+            barrier, inc=1, device_id=device(below, side, pair, core),
+            device_id_type=pl.DeviceIdType.MESH,
+        )
+
+    pl.semaphore_wait(barrier, 3 + has_above + has_below)
+
+    fetch.wait()
+
+    conditional = []
+    always = []
+
+    def start(copy):
+        always.append(copy)
+        copy.start()
+
+    def start_if(flag, copy):
+        conditional.append((flag, copy))
+
+        @pl.when(flag == 1)
+        def _():
+            copy.start()
+
+    def spread(z):
+        number = block(z, side, pair, core)
+        start(send(number, 0, other_pair))
+        start(send(number, 1, other_side))
+        start(send(number, 1, other_pair))
+        start(send(number, 0, other_side))
+        for h in (0, 1):
+            start(send(number, h, other_core))
+
+    own = block(plane, side, pair, core)
+    for h in (0, 1):
+        start_if(has_above, send(own, h, device(above, side, pair, core)))
+        start_if(has_below, send(own, h, device(below, side, pair, core)))
+    spread(plane)
+
+    def along(k):
+        z = table([orders[at][k] for at in range(planes)])
+        number = block(z, side, pair, core)
+        has, target = [], []
+        for at in range(planes):
+            onward = at + 1 if orders[at][k] < at else at - 1
+            has.append(1 if 0 <= onward < planes else 0)
+            target.append(min(max(onward, 0), planes - 1))
+        for h in (0, 1):
+            arrive(number, h)
+            start_if(table(has), send(number, h, device(table(target), side, pair, core)))
+        spread(z)
+        return z
+
+    def first_halves(z):
+        number = block(z, side, 1 - pair, core)
+        arrive(number, 0)
+        start(send(number, 0, other_side))
+        start(send(number, 0, other_core))
+        number = block(z, 1 - side, pair, core)
+        arrive(number, 1)
+        start(send(number, 1, other_pair))
+        start(send(number, 1, other_core))
+
+    me = expert * 4 + tensor
+    tile = slab.shape[1]
+    steps = width // tile
+    span = tile // columns
+    counted = jnp.zeros((1, 1), jnp.float32)
+
+    def accumulate(z, y, first, last, counted):
+        base = pl.multiple_of((z * 2 + y) * 4 * local, 4 * local)
+        picked[...] = rows[pl.ds(base, 4 * local), :]
+        named = picked[:, width:].astype(jnp.float32)
+        lane = lax.broadcasted_iota(jnp.int32, named.shape, 1)
+        chosen = jnp.sum(jnp.where(lane == me, named, 0.0), axis=1, keepdims=True)
+        source = picked
+        for bit in reversed(range(bits_ref.shape[0] // 2)):
+            shift, stay, go = 1 << bit, bits_ref[2 * bit], bits_ref[2 * bit + 1]
+
+            wanted = span + shift - 1
+            both = wanted if source is moved else min(wanted, width // columns - shift)
+
+            @pl.loop(0, both)
+            def _(j):
+                here = pl.ds(pl.multiple_of(j * columns, columns), columns)
+                there = pl.ds(pl.multiple_of((j + shift) * columns, columns), columns)
+                kept = source[:, here].reshape(-1, *stay.shape) * stay[None]
+                taken = source[:, there].reshape(-1, *stay.shape) * go[None]
+                moved[:, here] = (kept + taken).reshape(picked.shape[0], columns)
+
+            if both < wanted:
+                ends = slice(both * columns, wanted * columns)
+                moved[:, ends] = source[:, ends]
+
+            source = moved
+        slab[...] = (source[:, :tile].astype(jnp.float32) * chosen).astype(jnp.bfloat16)
+        counted = counted + jnp.sum(chosen, axis=0, keepdims=True)
+        factor = 2.0 / counted
+
+        @pl.loop(0, steps)
+        def _(step):
+            at = pl.ds(pl.multiple_of(step * tile, tile), tile)
+            part = lax.dot_general(
+                picked[:, at], slab[...], (((0,), (0,)), ((), ())),
+                preferred_element_type=jnp.float32,
+            )
+            if first:
+                total[at, :] = part
+            elif not last:
+                total[at, :] += part
+            else:
+                staged[at, :] = ((total[at, :] + part) * factor).astype(jnp.bfloat16)
+                pltpu.make_async_copy(staged.at[at, :], out_ref.at[at, :], out_sem.at[step]).start()
+
+        return counted
+
+    seen = plane
+    pending = None
+    for k in range(planes):
+        if k == 0:
+            first_halves(seen)
+        following = along(k) if k + 1 < planes else None
+        if k > 0:
+            first_halves(seen)
+            counted = accumulate(pending, side, k == 1, False, counted)
+            counted = accumulate(pending, 1 - side, False, False, counted)
+        for number, h in (
+            (block(seen, side, 1 - pair, core), 1),
+            (block(seen, 1 - side, pair, core), 0),
+        ):
+            arrive(number, h)
+            start(send(number, h, other_core))
+        diagonal = block(seen, 1 - side, 1 - pair, core)
+        for h in (0, 1):
+            if k + 1 == planes and h == 0:
+                for x in (0, 1):
+                    number = block(seen, side, x, 1 - core)
+                    arrive(number, 0)
+                    arrive(number, 1)
+                counted = accumulate(seen, side, planes == 1, False, counted)
+            arrive(diagonal, h)
+            start(send(diagonal, h, other_core))
+        for y in (side, 1 - side):
+            for x in (0, 1):
+                if k + 1 < planes or y is not side:
+                    number = block(seen, y, x, 1 - core)
+                    arrive(number, 0)
+                    arrive(number, 1)
+        pending, seen = seen, following
+    accumulate(pending, 1 - side, False, True, counted)
+
+    for copy in always:
+        copy.wait_send()
+    for flag, copy in conditional:
+
+        @pl.when(flag == 1)
+        def _(copy=copy):
+            copy.wait_send()
+
+    @pl.loop(0, steps)
+    def _(step):
+        at = pl.ds(pl.multiple_of(step * tile, tile), tile)
+        pltpu.make_async_copy(staged.at[at, :], out_ref.at[at, :], out_sem.at[step]).wait()
+
+
+def gathered_gram(payload, routes, slab_block, columns):
+    count_expert, count_tensor = lax.axis_size("expert"), lax.axis_size("tensor")
+    experts, planes = count_expert * count_tensor, count_expert // 2
+    local, width = payload.shape
+    extra = -(-experts // 128) * 128
+    expert_ids = jnp.arange(extra, dtype=jnp.int32)
+    chosen = jnp.any(routes[:, :, None] == expert_ids[None, None, :], axis=1)
+    own = jnp.concatenate([payload, chosen.astype(jnp.bfloat16)], axis=1)
+    reach = width // columns - SLAB // columns
+    levels = max(1, reach.bit_length())
+    places = jnp.arange(levels)
+    digits = (slab_block[0] >> places) & 1
+    bits = jnp.stack([1 - digits, digits], axis=1).reshape(-1, 1, 1)
+    bits = jnp.broadcast_to(bits, (2 * levels, 16, columns)).astype(jnp.bfloat16)
+    most = SLAB // columns + 2 ** levels
+    sends = planes * 14 + 2 * (planes + 1)
+    return pl.pallas_call(
+        functools.partial(gram_kernel, planes, local, width, columns),
+        out_shape=jax.ShapeDtypeStruct((width, SLAB), jnp.bfloat16),
+        in_specs=[
+            pl.BlockSpec(memory_space=pltpu.VMEM),
+            pl.BlockSpec(memory_space=pl.ANY),
+        ],
+        out_specs=pl.BlockSpec(memory_space=pl.ANY),
+        scratch_shapes=[
+            pltpu.VMEM((experts * local, width + extra), jnp.bfloat16),
+            pltpu.VMEM((4 * local, width + extra), jnp.bfloat16),
+            pltpu.VMEM((4 * local, most * columns // 2 + SLAB), jnp.bfloat16),
+            pltpu.VMEM((4 * local, SLAB), jnp.bfloat16),
+            pltpu.VMEM((width, SLAB), jnp.float32),
+            pltpu.VMEM((width, SLAB), jnp.bfloat16),
+            pltpu.SemaphoreType.DMA,
+            pltpu.SemaphoreType.DMA((sends,)),
+            pltpu.SemaphoreType.DMA((experts, 2)),
+            pltpu.SemaphoreType.DMA((width // SLAB,)),
+        ],
+        compiler_params=pltpu.CompilerParams(
+            collective_id=0, has_side_effects=True, vmem_limit_bytes=67043328
+        ),
+        name="gathered_gram",
+    )(bits, own)
 
 
 def on_device(attn_partial, residual, norm_gain, channel_order, rotation, routes, slab_block):
@@ -78,13 +371,10 @@
     mean_load = residual.shape[0] * routes.shape[1] // experts
     slots = max(2, mean_load + (mean_load + 1) // 2)
     start = slab_block[0] * rotation.shape[1]
-    if residual.shape[0] <= 4 * slots:
-        rows, chosen, count = gather_rows(payload, routes)
-        slab = lax.dynamic_slice_in_dim(rows, start, SLAB, 1)
-        slab = slab * chosen[:, None].astype(slab.dtype)
-    else:
-        rows, count = dispatch_rows(payload, routes)
-        slab = lax.dynamic_slice_in_dim(rows, start, SLAB, 1)
+    if residual.shape[0] <= 4 * slots and lax.axis_size("tensor") == 4:
+        return gathered_gram(payload, routes, slab_block, rotation.shape[1])[None]
+    rows, count = dispatch_rows(payload, routes)
+    slab = lax.dynamic_slice_in_dim(rows, start, SLAB, 1)
     product = lax.dot_general(
         rows, slab, (((0,), (0,)), ((), ())), preferred_element_type=jnp.float32
     )

time: 295 us -> 274 us (0.929)
  Pallas kernels: 0 us -> 173 us
  waiting for transfers between devices: 178 us -> 46.1 us
  blocking collectives: 42.1 us -> 0 us
  matrix products: 24.2 us -> 0.6 us
  local copies, waits for them, and re-layouts: 32.1 us -> 36.5 us
    pallas_call x0 -> x1, Pallas kernels: none -> 173 us  [gathered_gram(): pl.pallas_call(functools.partial(gram_kernel, planes, local, width, colum...]
    all_gather x1 -> x0, waiting for transfers between devices: 131 us -> none  [gather_rows(): rows = lax.all_gather(payload, ('expert', 'tensor'), axis=0, tiled=True)]
    all_gather x1 -> x0, blocking collectives: 42.1 us -> none  [gather_rows(): named = lax.all_gather(routes, ('expert', 'tensor'), axis=0, tiled=True)]
    dot_general x1 -> x0, matrix products: 23.6 us -> none  [on_device(): lax.dot_general(rows, slab, (((0,), (0,)), ((), ())), preferred_element_t...]
    unnamed x12 -> x14, local copies, waits for them, and re-layouts: 0.13 us -> 6.74 us
  transfers between devices with their start and end apart: 2 -> 1, of which waited for: 2 -> 1; matrix products, arithmetic and copies ran while one was open for 0% -> 0% of each run, Pallas kernels for 0% -> 0%
where the time goes in v2:
time: 274 us
  Pallas kernels  173 us (63%)
  waiting for transfers between devices  46.1 us (17%)
  local copies, waits for them, and re-layouts  36.5 us (13%)
  between operations  14.2 us (5%)
  other arithmetic  3.24 us (1%)
    pallas_call x1, Pallas kernels, gathered_gram(): pl.pallas_call(functools.partial(gram_kernel, planes, local, width, colum...  173 us
    reduce_scatter x1, waiting for transfers between devices, on_device(): lax.psum_scatter(attn_partial[0].astype(jnp.float32).astype(jnp.bfloat16)...  45.4 us
    gather x2, local copies, waits for them, and re-layouts, rotate_rows(): moved = jnp.take(rows, channel_order, axis=1)  27.8 us
    unnamed x14, local copies, waits for them, and re-layouts  6.74 us
  transfers between devices with their start and end apart: 1, of which 1 were waited for; matrix products, arithmetic and copies ran while one was open for 0% of the time, Pallas kernels for 0%

profile of v2, /device:TPU:0, one launch (start us, length us, event | category | flops | bytes accessed | tf_op | source)
XLA Modules:
  0.0 273.9 jit_solution(14816510002192457462)
XLA Ops:
  6.5 0.0 reduce-scatter.4.cloned.1.call-start
  6.5 0.7 reduce-scatter.4.cloned.1.call-update
  7.3 0.0 copy-start.4
  7.9 0.1 copy.30
  8.1 0.1 convert_element_type.26
  8.1 0.0 copy-done.5
  8.1 0.1 copy.36
  8.2 0.2 fusion.4
  8.4 0.0 copy-done.3
  8.5 45.4 %reduce-scatter.4.cloned.1.call-done = bf16[64,7168]{1,0:T(8,128)(2,1)} async-done(((bf16[256,7168]{1,0:T(8,128)(2,1)}), bf16[64,7168]{1,0:T(8,128)(2,1)}) %reduce-scatter.4.cloned.1.call-update) | async-done | bytes 917520 | tf_op jit(solution)/shard_map/reduce_scatter | solution.py:360
  53.9 0.0 copy-done
  53.9 1.7 multiply_reduce_fusion
  55.5 0.0 copy-done.4
  55.6 0.4 multiply_convert_fusion
  55.9 1.0 copy.33
  56.9 25.8 %gather_fusion = bf16[7168,64]{1,0:T(8,128)(2,1)} fusion(bf16[64,7168]{0,1:T(8,128)(2,1)S(1)} %copy.33, s32[7168]{0:T(1024)S(1)} %fusion.5), kind=kCustom, calls=%fused_computation | custom fusion | bytes 1863680 | tf_op jit(solution)/shard_map/jit(_take)/gather | solution.py:14
  82.7 2.0 copy.34
  84.7 0.0 copy-done.2
  84.7 0.6 fusion
  85.3 0.2 copy.42
  85.5 1.0 pad_maximum_fusion.own_ref
  86.5 0.7 broadcast_in_dim.26.bits_ref
  87.2 173.2 %gathered_gram.1 = bf16[7168,512]{1,0:T(8,128)(2,1)} custom-call(bf16[12,16,128]{2,1,0:T(8,128)(2,1)} %broadcast_in_dim.26.bits_ref, bf16[64,7296]{1,0:T(8,128)(2,1)} %pad_maximum_fusion.own_ref), custom_call_target="tpu_custom_call" | custom-call | tf_op jit(solution)/shard_map/gathered_gram/pallas_call | solution.py:332
  260.4 6.6 %copy.45 = bf16[1,7168,512]{2,1,0:T(8,128)(2,1)} copy(bf16[1,7168,512]{2,1,0:T(8,128)(2,1)} %bitcast.18) | data formatting | bytes 14680064
  (12 shorter events, 0.1 us)
Async XLA Ops:
  6.5 47.3 %reduce-scatter.4.cloned.1.call-start = ((), (), s32[]{:S(2)}) async-start(), calls=%async_computation.1 | async-start | bytes 4587520 | tf_op jit(solution)/shard_map/reduce_scatter | solution.py:360
  6.5 1.6 copy-start.5
  6.5 1.9 copy-start.3
  6.5 47.3 %copy-start = (bf16[64,7168]{1,0:T(8,128)(2,1)S(1)}, bf16[64,7168]{1,0:T(8,128)(2,1)}, u32[]{:S(2)}) copy-start(bf16[64,7168]{1,0:T(8,128)(2,1)} %param.8) | copy-start | bytes 2752516
  7.3 48.3 %copy-start.4 = (f32[7168]{0:T(1024)S(1)}, f32[7168]{0:T(1024)}, u32[]{:S(2)}) copy-start(f32[7168]{0:T(1024)} %param.9) | copy-start | bytes 86020
  53.9 1.7 copy-start.1
  82.7 2.1 copy-start.2
Sparse Core Ops, SparseCore 0:
  9.9 43.9 reduce-scatter.3

commit v3 on v2

--- a/solution.py
+++ b/solution.py
@@ -122,10 +122,9 @@
     other_pair = device(plane, side, 1 - pair, core)
     other_side = device(plane, 1 - side, pair, core)
     other_core = device(plane, side, pair, 1 - core)
-    has_above = table([1 if at + 1 < planes else 0 for at in range(planes)])
-    has_below = table([1 if at >= 1 else 0 for at in range(planes)])
-    above = table([min(at + 1, planes - 1) for at in range(planes)])
-    below = table([max(at - 1, 0) for at in range(planes)])
+    planes_by_turn = [
+        table([orders[at][k] for at in range(planes)]) for k in range(planes - 1)
+    ]
 
     fetch = pltpu.make_async_copy(
         own_ref,
@@ -135,81 +134,47 @@
     fetch.start()
 
     barrier = pltpu.get_barrier_semaphore()
-    for peer in (other_pair, other_side, other_core):
+    peers = [other_pair, other_side, other_core]
+    peers += [device(z, side, pair, core) for z in planes_by_turn]
+    for peer in peers:
         pl.semaphore_signal(
             barrier, inc=1, device_id=peer, device_id_type=pl.DeviceIdType.MESH
         )
-
-    @pl.when(has_above == 1)
-    def _():
-        pl.semaphore_signal(
-            barrier, inc=1, device_id=device(above, side, pair, core),
-            device_id_type=pl.DeviceIdType.MESH,
-        )
-
-    @pl.when(has_below == 1)
-    def _():
-        pl.semaphore_signal(
-            barrier, inc=1, device_id=device(below, side, pair, core),
-            device_id_type=pl.DeviceIdType.MESH,
-        )
-
-    pl.semaphore_wait(barrier, 3 + has_above + has_below)
+    pl.semaphore_wait(barrier, len(peers))
 
     fetch.wait()
-
-    conditional = []
-    always = []
-
-    def start(copy):
-        always.append(copy)
-        copy.start()
-
-    def start_if(flag, copy):
-        conditional.append((flag, copy))
-
-        @pl.when(flag == 1)
-        def _():
-            copy.start()
 
     def spread(z):
         number = block(z, side, pair, core)
-        start(send(number, 0, other_pair))
-        start(send(number, 1, other_side))
-        start(send(number, 1, other_pair))
-        start(send(number, 0, other_side))
+        send(number, 0, other_pair).start()
+        send(number, 1, other_side).start()
+        send(number, 1, other_pair).start()
+        send(number, 0, other_side).start()
         for h in (0, 1):
-            start(send(number, h, other_core))
+            send(number, h, other_core).start()
 
     own = block(plane, side, pair, core)
-    for h in (0, 1):
-        start_if(has_above, send(own, h, device(above, side, pair, core)))
-        start_if(has_below, send(own, h, device(below, side, pair, core)))
     spread(plane)
+    for z in planes_by_turn:
+        for h in (0, 1):
+            send(own, h, device(z, side, pair, core)).start()
 
     def along(k):
-        z = table([orders[at][k] for at in range(planes)])
-        number = block(z, side, pair, core)
-        has, target = [], []
-        for at in range(planes):
-            onward = at + 1 if orders[at][k] < at else at - 1
-            has.append(1 if 0 <= onward < planes else 0)
-            target.append(min(max(onward, 0), planes - 1))
+        z = planes_by_turn[k]
         for h in (0, 1):
-            arrive(number, h)
-            start_if(table(has), send(number, h, device(table(target), side, pair, core)))
+            arrive(block(z, side, pair, core), h)
         spread(z)
         return z
 
     def first_halves(z):
         number = block(z, side, 1 - pair, core)
         arrive(number, 0)
-        start(send(number, 0, other_side))
-        start(send(number, 0, other_core))
+        send(number, 0, other_side).start()
+        send(number, 0, other_core).start()
         number = block(z, 1 - side, pair, core)
         arrive(number, 1)
-        start(send(number, 1, other_pair))
-        start(send(number, 1, other_core))
+        send(number, 1, other_pair).start()
+        send(number, 1, other_core).start()
 
     me = expert * 4 + tensor
     tile = slab.shape[1]
@@ -264,48 +229,38 @@
 
         return counted
 
-    seen = plane
-    pending = None
+    def from_other_core(z, y):
+        for x in (0, 1):
+            for h in (0, 1):
+                arrive(block(z, y, x, 1 - core), h)
+
+    seen, before = plane, None
     for k in range(planes):
-        if k == 0:
-            first_halves(seen)
+        first_halves(seen)
+        if k > 0:
+            counted = accumulate(before, 1 - side, False, False, counted)
         following = along(k) if k + 1 < planes else None
-        if k > 0:
-            first_halves(seen)
-            counted = accumulate(pending, side, k == 1, False, counted)
-            counted = accumulate(pending, 1 - side, False, False, counted)
         for number, h in (
             (block(seen, side, 1 - pair, core), 1),
             (block(seen, 1 - side, pair, core), 0),
         ):
             arrive(number, h)
-            start(send(number, h, other_core))
-        diagonal = block(seen, 1 - side, 1 - pair, core)
+            send(number, h, other_core).start()
+        from_other_core(seen, side)
+        if k + 1 == planes:
+            counted = accumulate(seen, side, k == 0, False, counted)
         for h in (0, 1):
-            if k + 1 == planes and h == 0:
-                for x in (0, 1):
-                    number = block(seen, side, x, 1 - core)
-                    arrive(number, 0)
-                    arrive(number, 1)
-                counted = accumulate(seen, side, planes == 1, False, counted)
-            arrive(diagonal, h)
-            start(send(diagonal, h, other_core))
-        for y in (side, 1 - side):
-            for x in (0, 1):
-                if k + 1 < planes or y is not side:
-                    number = block(seen, y, x, 1 - core)
-                    arrive(number, 0)
-                    arrive(number, 1)
-        pending, seen = seen, following
-    accumulate(pending, 1 - side, False, True, counted)
-
-    for copy in always:
+            number = block(seen, 1 - side, 1 - pair, core)
+            arrive(number, h)
+            send(number, h, other_core).start()
+        from_other_core(seen, 1 - side)
+        if k + 1 < planes:
+            counted = accumulate(seen, side, k == 0, False, counted)
+        before, seen = seen, following
+    accumulate(before, 1 - side, False, True, counted)
+
+    for copy in sends:
         copy.wait_send()
-    for flag, copy in conditional:
-
-        @pl.when(flag == 1)
-        def _(copy=copy):
-            copy.wait_send()
 
     @pl.loop(0, steps)
     def _(step):
@@ -328,7 +283,7 @@
     bits = jnp.stack([1 - digits, digits], axis=1).reshape(-1, 1, 1)
     bits = jnp.broadcast_to(bits, (2 * levels, 16, columns)).astype(jnp.bfloat16)
     most = SLAB // columns + 2 ** levels
-    sends = planes * 14 + 2 * (planes + 1)
+    sends = planes * 14 + 2 * (planes - 1)
     return pl.pallas_call(
         functools.partial(gram_kernel, planes, local, width, columns),
         out_shape=jax.ShapeDtypeStruct((width, SLAB), jnp.bfloat16),

time: 274 us -> 258 us (0.942)
  Pallas kernels: 173 us -> 156 us
    pallas_call x1, Pallas kernels: 173 us -> 156 us  [gathered_gram(): pl.pallas_call(functools.partial(gram_kernel, planes, local, width, colum...]
where the time goes in v3:
time: 258 us; the launch traced here: 257 us
  Pallas kernels  156 us (60%)
  waiting for transfers between devices  46.1 us (18%)
  local copies, waits for them, and re-layouts  36.5 us (14%)
  between operations  14.2 us (6%)
  other arithmetic  3.24 us (1%)
    pallas_call x1, Pallas kernels, gathered_gram(): pl.pallas_call(functools.partial(gram_kernel, planes, local, width, colum...  156 us
    reduce_scatter x1, waiting for transfers between devices, on_device(): lax.psum_scatter(attn_partial[0].astype(jnp.float32).astype(jnp.bfloat16)...  45.4 us
    gather x2, local copies, waits for them, and re-layouts, rotate_rows(): moved = jnp.take(rows, channel_order, axis=1)  27.8 us
    unnamed x14, local copies, waits for them, and re-layouts  6.74 us
  transfers between devices with their start and end apart: 1, of which 1 were waited for; matrix products, arithmetic and copies ran while one was open for 0% of the time, Pallas kernels for 0%

profile of v3, /device:TPU:0, one launch (start us, length us, event | category | flops | bytes accessed | tf_op | source)
XLA Modules:
  0.0 256.9 jit_solution(6170478574716157724)
XLA Ops:
  6.5 0.0 reduce-scatter.4.cloned.1.call-start
  6.5 0.7 reduce-scatter.4.cloned.1.call-update
  7.3 0.0 copy-start.4
  7.9 0.1 copy.30
  8.1 0.1 convert_element_type.26
  8.1 0.0 copy-done.5
  8.1 0.1 copy.36
  8.2 0.2 fusion.4
  8.4 0.0 copy-done.3
  8.5 45.4 %reduce-scatter.4.cloned.1.call-done = bf16[64,7168]{1,0:T(8,128)(2,1)} async-done(((bf16[256,7168]{1,0:T(8,128)(2,1)}), bf16[64,7168]{1,0:T(8,128)(2,1)}) %reduce-scatter.4.cloned.1.call-update) | async-done | bytes 917520 | tf_op jit(solution)/shard_map/reduce_scatter | solution.py:315
  53.9 0.0 copy-done
  53.9 1.7 multiply_reduce_fusion
  55.5 0.0 copy-done.4
  55.6 0.4 multiply_convert_fusion
  55.9 1.0 copy.33
  56.9 25.8 %gather_fusion = bf16[7168,64]{1,0:T(8,128)(2,1)} fusion(bf16[64,7168]{0,1:T(8,128)(2,1)S(1)} %copy.33, s32[7168]{0:T(1024)S(1)} %fusion.5), kind=kCustom, calls=%fused_computation | custom fusion | bytes 1863680 | tf_op jit(solution)/shard_map/jit(_take)/gather | solution.py:14
  82.7 2.0 copy.34
  84.7 0.0 copy-done.2
  84.7 0.6 fusion
  85.3 0.2 copy.42
  85.5 1.0 pad_maximum_fusion.own_ref
  86.5 0.7 broadcast_in_dim.26.bits_ref
  87.2 156.2 %gathered_gram.1 = bf16[7168,512]{1,0:T(8,128)(2,1)} custom-call(bf16[12,16,128]{2,1,0:T(8,128)(2,1)} %broadcast_in_dim.26.bits_ref, bf16[64,7296]{1,0:T(8,128)(2,1)} %pad_maximum_fusion.own_ref), custom_call_target="tpu_custom_call" | custom-call | tf_op jit(solution)/shard_map/gathered_gram/pallas_call | solution.py:287
  243.4 6.6 %copy.45 = bf16[1,7168,512]{2,1,0:T(8,128)(2,1)} copy(bf16[1,7168,512]{2,1,0:T(8,128)(2,1)} %bitcast.18) | data formatting | bytes 14680064
  (12 shorter events, 0.1 us)
Async XLA Ops:
  6.5 47.3 %reduce-scatter.4.cloned.1.call-start = ((), (), s32[]{:S(2)}) async-start(), calls=%async_computation.1 | async-start | bytes 4587520 | tf_op jit(solution)/shard_map/reduce_scatter | solution.py:315
  6.5 1.6 copy-start.5
  6.5 1.9 copy-start.3
  6.5 47.3 %copy-start = (bf16[64,7168]{1,0:T(8,128)(2,1)S(1)}, bf16[64,7168]{1,0:T(8,128)(2,1)}, u32[]{:S(2)}) copy-start(bf16[64,7168]{1,0:T(8,128)(2,1)} %param.8) | copy-start | bytes 2752516
  7.3 48.3 %copy-start.4 = (f32[7168]{0:T(1024)S(1)}, f32[7168]{0:T(1024)}, u32[]{:S(2)}) copy-start(f32[7168]{0:T(1024)} %param.9) | copy-start | bytes 86020
  53.9 1.7 copy-start.1
  82.7 2.1 copy-start.2
Sparse Core Ops, SparseCore 0:
  9.9 43.9 reduce-scatter.3

commit v4 on v3

--- a/solution.py
+++ b/solution.py
@@ -101,7 +101,7 @@
         copy = pltpu.make_async_remote_copy(
             src_ref=piece(number, h),
             dst_ref=piece(number, h),
-            send_sem=send_sem.at[len(sends)],
+            send_sem=send_sem.at[len(sends) + len(conditional)],
             recv_sem=recv_sem.at[number, h],
             device_id=target,
             device_id_type=pl.DeviceIdType.MESH,
@@ -126,6 +126,21 @@
         table([orders[at][k] for at in range(planes)]) for k in range(planes - 1)
     ]
 
+    def beside(step):
+        there = table([1 if 0 <= at + step < planes else 0 for at in range(planes)])
+        return there, table([min(max(at + step, 0), planes - 1) for at in range(planes)])
+
+    conditional = []
+
+    def send_if(flag, number, h, z):
+        copy = send(number, h, device(z, side, pair, core))
+        sends.pop()
+        conditional.append((flag, copy))
+
+        @pl.when(flag == 1)
+        def _():
+            copy.start()
+
     fetch = pltpu.make_async_copy(
         own_ref,
         rows.at[pl.ds(pl.multiple_of(block(plane, side, pair, core) * local, local), local), :],
@@ -134,13 +149,23 @@
     fetch.start()
 
     barrier = pltpu.get_barrier_semaphore()
-    peers = [other_pair, other_side, other_core]
-    peers += [device(z, side, pair, core) for z in planes_by_turn]
-    for peer in peers:
+    barrier_wait = 3
+    for peer in (other_pair, other_side, other_core):
         pl.semaphore_signal(
             barrier, inc=1, device_id=peer, device_id_type=pl.DeviceIdType.MESH
         )
-    pl.semaphore_wait(barrier, len(peers))
+    for step in (-1, 1):
+        there, z = beside(step)
+        barrier_wait = barrier_wait + there
+
+        @pl.when(there == 1)
+        def _():
+            pl.semaphore_signal(
+                barrier, inc=1, device_id=device(z, side, pair, core),
+                device_id_type=pl.DeviceIdType.MESH,
+            )
+
+    pl.semaphore_wait(barrier, barrier_wait)
 
     fetch.wait()
 
@@ -155,14 +180,27 @@
 
     own = block(plane, side, pair, core)
     spread(plane)
-    for z in planes_by_turn:
+    for h in (0, 1):
+        for step in (-1, 1):
+            there, z = beside(step)
+            send_if(there, own, h, z)
+
+    def take(far):
         for h in (0, 1):
-            send(own, h, device(z, side, pair, core)).start()
+            for step in (-1, 1):
+                there, z = beside(step * far)
+                onward, target = beside(-step)
+                number = block(z, side, pair, core)
+
+                @pl.when(there == 1)
+                def _():
+                    arrive(number, h)
+
+                send_if(there * onward, number, h, target)
 
     def along(k):
+        take(k + 1)
         z = planes_by_turn[k]
-        for h in (0, 1):
-            arrive(block(z, side, pair, core), h)
         spread(z)
         return z
 
@@ -261,6 +299,11 @@
 
     for copy in sends:
         copy.wait_send()
+    for flag, copy in conditional:
+
+        @pl.when(flag == 1)
+        def _(copy=copy):
+            copy.wait_send()
 
     @pl.loop(0, steps)
     def _(step):
@@ -283,7 +326,7 @@
     bits = jnp.stack([1 - digits, digits], axis=1).reshape(-1, 1, 1)
     bits = jnp.broadcast_to(bits, (2 * levels, 16, columns)).astype(jnp.bfloat16)
     most = SLAB // columns + 2 ** levels
-    sends = planes * 14 + 2 * (planes - 1)
+    sends = planes * 14 + planes * 4
     return pl.pallas_call(
         functools.partial(gram_kernel, planes, local, width, columns),
         out_shape=jax.ShapeDtypeStruct((width, SLAB), jnp.bfloat16),
@@ -311,22 +354,138 @@
     )(bits, own)
 
 
+def normed_kernel(
+    local, partial_ref, residual_ref, gain_ref, out_ref,
+    mine, got, mid, far, own_sem, core_send, core_recv, pair_send, pair_recv,
+):
+    expert, tensor = lax.axis_index("expert"), lax.axis_index("tensor")
+    pair, core = lax.div(tensor, 2), lax.rem(tensor, 2)
+    other_core = (expert, pair * 2 + 1 - core)
+    other_pair = (expert, (1 - pair) * 2 + core)
+    parts = 4
+    size = local // parts
+
+    def source(p, c, at, count):
+        start = pl.multiple_of((p * 2 + c) * local + at, size)
+        return partial_ref.at[0, pl.ds(start, count), :]
+
+    loads = []
+    for turn, p in enumerate((1 - pair, pair)):
+        loads.append(pltpu.make_async_copy(source(p, core, 0, local), mine.at[turn], own_sem.at[turn]))
+        loads[-1].start()
+
+    barrier = pltpu.get_barrier_semaphore()
+    for peer in (other_core, other_pair):
+        pl.semaphore_signal(
+            barrier, inc=1, device_id=peer, device_id_type=pl.DeviceIdType.MESH
+        )
+    pl.semaphore_wait(barrier, 2)
+
+    inside = []
+    for turn, p in enumerate((1 - pair, pair)):
+        for part in range(parts):
+            rows = pl.ds(part * size, size)
+            number = turn * parts + part
+            inside.append(
+                pltpu.make_async_remote_copy(
+                    src_ref=source(p, 1 - core, part * size, size),
+                    dst_ref=got.at[turn, rows, :],
+                    send_sem=core_send.at[number],
+                    recv_sem=core_recv.at[number],
+                    device_id=other_core,
+                    device_id_type=pl.DeviceIdType.MESH,
+                )
+            )
+            inside[-1].start()
+
+    across = []
+    loads[0].wait()
+    for part in range(parts):
+        rows = pl.ds(part * size, size)
+        inside[part].wait_recv()
+        mid[rows, :] = (
+            mine[0, rows, :].astype(jnp.float32) + got[0, rows, :].astype(jnp.float32)
+        ).astype(jnp.bfloat16)
+        across.append(
+            pltpu.make_async_remote_copy(
+                src_ref=mid.at[rows, :],
+                dst_ref=far.at[rows, :],
+                send_sem=pair_send.at[part],
+                recv_sem=pair_recv.at[part],
+                device_id=other_pair,
+                device_id_type=pl.DeviceIdType.MESH,
+            )
+        )
+        if part > 0:
+            across[part - 1].start()
+    loads[1].wait()
+    for part in range(parts):
+        inside[parts + part].wait_recv()
+    across[parts - 1].start()
+
+    for part in range(parts):
+        rows = pl.ds(part * size, size)
+        across[part].wait_recv()
+        attn = (
+            mine[1, rows, :].astype(jnp.float32)
+            + got[1, rows, :].astype(jnp.float32)
+            + far[rows, :].astype(jnp.float32)
+        )
+        hidden = residual_ref[rows, :].astype(jnp.float32) + attn
+        scale = lax.rsqrt(jnp.mean(hidden * hidden, axis=1, keepdims=True) + 1e-06)
+        out_ref[rows, :] = (hidden * scale * gain_ref[...]).astype(jnp.bfloat16)
+
+    for copy in inside + across:
+        copy.wait_send()
+
+
+def normed_rows(attn_partial, residual, norm_gain):
+    local, width = residual.shape
+    return pl.pallas_call(
+        functools.partial(normed_kernel, local),
+        out_shape=jax.ShapeDtypeStruct((local, width), jnp.bfloat16),
+        in_specs=[
+            pl.BlockSpec(memory_space=pl.ANY),
+            pl.BlockSpec(memory_space=pltpu.VMEM),
+            pl.BlockSpec(memory_space=pltpu.VMEM),
+        ],
+        out_specs=pl.BlockSpec(memory_space=pltpu.VMEM),
+        scratch_shapes=[
+            pltpu.VMEM((2, local, width), jnp.bfloat16),
+            pltpu.VMEM((2, local, width), jnp.bfloat16),
+            pltpu.VMEM((local, width), jnp.bfloat16),
+            pltpu.VMEM((local, width), jnp.bfloat16),
+            pltpu.SemaphoreType.DMA((2,)),
+            pltpu.SemaphoreType.DMA((8,)),
+            pltpu.SemaphoreType.DMA((8,)),
+            pltpu.SemaphoreType.DMA((4,)),
+            pltpu.SemaphoreType.DMA((4,)),
+        ],
+        compiler_params=pltpu.CompilerParams(collective_id=1, has_side_effects=True),
+        name="normed_rows",
+    )(attn_partial, residual, norm_gain[None, :])
+
+
 def on_device(attn_partial, residual, norm_gain, channel_order, rotation, routes, slab_block):
-    summed = lax.psum_scatter(
-        attn_partial[0].astype(jnp.float32).astype(jnp.bfloat16),
-        "tensor",
-        scatter_dimension=0,
-        tiled=True,
-    ).astype(jnp.float32)
-    hidden = residual.astype(jnp.float32) + summed
-    scale = lax.rsqrt(jnp.mean(hidden * hidden, axis=1, keepdims=True) + 1e-06)
-    normed = (hidden * scale * norm_gain[None, :]).astype(jnp.bfloat16)
-    payload = rotate_rows(normed, channel_order, rotation)
     experts = lax.axis_size("expert") * lax.axis_size("tensor")
     mean_load = residual.shape[0] * routes.shape[1] // experts
     slots = max(2, mean_load + (mean_load + 1) // 2)
+    spread_all = residual.shape[0] <= 4 * slots and lax.axis_size("tensor") == 4
+    if spread_all:
+        normed = normed_rows(attn_partial, residual, norm_gain)
+    else:
+        summed = lax.psum_scatter(
+            attn_partial[0].astype(jnp.float32).astype(jnp.bfloat16),
+            "tensor",
+            scatter_dimension=0,
+            tiled=True,
+        ).astype(jnp.float32)
+        hidden = residual.astype(jnp.float32) + summed
+        scale = lax.rsqrt(jnp.mean(hidden * hidden, axis=1, keepdims=True) + 1e-06)
+        normed = (hidden * scale * norm_gain[None, :]).astype(jnp.bfloat16)
+    payload = rotate_rows(normed, channel_order, rotation)
     start = slab_block[0] * rotation.shape[1]
-    if residual.shape[0] <= 4 * slots and lax.axis_size("tensor") == 4:
+    if spread_all:
         return gathered_gram(payload, routes, slab_block, rotation.shape[1])[None]
     rows, count = dispatch_rows(payload, routes)
     slab = lax.dynamic_slice_in_dim(rows, start, SLAB, 1)

time: 258 us -> 207 us (0.80)
  waiting for transfers between devices: 46.1 us -> 0 us
  between operations: 14.2 us -> 0.73 us
  Pallas kernels: 156 us -> 163 us
    reduce_scatter x1 -> x0, waiting for transfers between devices: 45.4 us -> none  [on_device(): lax.psum_scatter(attn_partial[0].astype(jnp.float32).astype(jnp.bfloat16)...]
    pallas_call x0 -> x1, Pallas kernels: none -> 28.2 us  [normed_rows(): pl.pallas_call(functools.partial(normed_kernel, local), out_shape=jax.Sha...]
    pallas_call x1, Pallas kernels: 156 us -> 135 us  [gathered_gram(): pl.pallas_call(functools.partial(gram_kernel, planes, local, width, colum...]
    unnamed x14 -> x4, local copies, waits for them, and re-layouts: 6.74 us -> 7.41 us
  transfers between devices with their start and end apart: 1 -> 0, of which waited for: 1 -> 0; matrix products, arithmetic and copies ran while one was open for 0% -> 0% of each run, Pallas kernels for 0% -> 0%
where the time goes in v4:
time: 207 us; the launch traced here: 205 us
  Pallas kernels  163 us (79%)
  local copies, waits for them, and re-layouts  38.1 us (18%)
  other arithmetic  2.71 us (1%)
    pallas_call x1, Pallas kernels, gathered_gram(): pl.pallas_call(functools.partial(gram_kernel, planes, local, width, colum...  135 us
    pallas_call x1, Pallas kernels, normed_rows(): pl.pallas_call(functools.partial(normed_kernel, local), out_shape=jax.Sha...  28.2 us
    gather x2, local copies, waits for them, and re-layouts, rotate_rows(): moved = jnp.take(rows, channel_order, axis=1)  27.8 us
    unnamed x4, local copies, waits for them, and re-layouts  7.41 us

profile of v4, /device:TPU:0, one launch (start us, length us, event | category | flops | bytes accessed | tf_op | source)
XLA Modules:
  0.0 205.2 jit_solution(9721508935100612901)
XLA Ops:
  0.7 0.1 copy.21
  0.8 0.1 convert_element_type.15
  0.9 0.8 and_bitcast_fusion
  1.6 0.8 fusion.5
  2.4 0.8 copy.25
  3.2 0.2 fusion.4
  3.4 0.7 broadcast_in_dim.27.bits_ref
  4.1 28.2 %normed_rows.1 = bf16[64,7168]{1,0:T(8,128)(2,1)} custom-call(bf16[1,256,7168]{2,1,0:T(8,128)(2,1)} %partial_ref.1, bf16[64,7168]{1,0:T(8,128)(2,1)} %residual_ref.1, f32[1,7168]{1,0:T(1,128)} %bitcast.19), custom_call_target="tpu_custom_call" | custom-call | tf_op jit(solution)/shard_map/normed_rows/pallas_call | solution.py:444
  32.2 1.9 copy.22
  34.1 25.8 %gather_fusion = bf16[7168,64]{1,0:T(8,128)(2,1)} fusion(bf16[64,7168]{0,1:T(8,128)(2,1)S(1)} %copy.22, s32[7168]{0:T(1024)S(1)} %fusion.5), kind=kCustom, calls=%fused_computation | custom fusion | bytes 1863680 | tf_op jit(solution)/shard_map/jit(_take)/gather | solution.py:14
  59.9 0.0 copy-start
  59.9 2.0 copy.23
  61.9 0.0 copy-done
  61.9 0.6 fusion
  62.6 0.2 copy.28
  62.7 1.0 pad_maximum_fusion.own_ref
  63.7 134.9 %gathered_gram.1 = bf16[7168,512]{1,0:T(8,128)(2,1)} custom-call(bf16[12,16,128]{2,1,0:T(8,128)(2,1)} %broadcast_in_dim.27.bits_ref, bf16[64,7296]{1,0:T(8,128)(2,1)} %pad_maximum_fusion.own_ref), custom_call_target="tpu_custom_call" | custom-call | tf_op jit(solution)/shard_map/gathered_gram/pallas_call | solution.py:330
  198.6 6.6 %copy.31 = bf16[1,7168,512]{2,1,0:T(8,128)(2,1)} copy(bf16[1,7168,512]{2,1,0:T(8,128)(2,1)} %bitcast.16) | data formatting | bytes 14680064
  (3 shorter events, 0.0 us)
Async XLA Ops:
  59.9 2.1 copy-start

commit v5 on v4

--- a/solution.py
+++ b/solution.py
@@ -466,6 +466,49 @@
     )(attn_partial, residual, norm_gain[None, :])
 
 
+def rotated_kernel(order_ref, rows_ref, rotation_ref, out_ref, flipped, moved):
+    size = rotation_ref.shape[1]
+    group = 32
+
+    @pl.loop(0, rotation_ref.shape[0])
+    def _(b):
+        at = pl.ds(pl.multiple_of(b * size, size), size)
+        flipped[at, :] = rows_ref[:, at].astype(jnp.float32).T
+
+    @pl.loop(0, flipped.shape[0] // group)
+    def _(step):
+        base = pl.multiple_of(step * group, group)
+        for j in range(group):
+            moved[pl.ds(base + j, 1), :] = flipped[pl.ds(order_ref[base + j], 1), :]
+
+    @pl.loop(0, rotation_ref.shape[0])
+    def _(b):
+        at = pl.ds(pl.multiple_of(b * size, size), size)
+        out_ref[:, at] = lax.dot_general(
+            moved[at, :].T.astype(jnp.bfloat16), rotation_ref[b], (((1,), (0,)), ((), ())),
+            preferred_element_type=jnp.float32,
+        ).astype(jnp.bfloat16)
+
+
+def rotated_rows(rows, channel_order, rotation):
+    local, width = rows.shape
+    return pl.pallas_call(
+        rotated_kernel,
+        out_shape=jax.ShapeDtypeStruct((local, width), jnp.bfloat16),
+        in_specs=[
+            pl.BlockSpec(memory_space=pltpu.SMEM),
+            pl.BlockSpec(memory_space=pltpu.VMEM),
+            pl.BlockSpec(memory_space=pltpu.VMEM),
+        ],
+        out_specs=pl.BlockSpec(memory_space=pltpu.VMEM),
+        scratch_shapes=[
+            pltpu.VMEM((width, local), jnp.float32),
+            pltpu.VMEM((width, local), jnp.float32),
+        ],
+        name="rotated_rows",
+    )(channel_order, rows, rotation)
+
+
 def on_device(attn_partial, residual, norm_gain, channel_order, rotation, routes, slab_block):
     experts = lax.axis_size("expert") * lax.axis_size("tensor")
     mean_load = residual.shape[0] * routes.shape[1] // experts
@@ -473,6 +516,7 @@
     spread_all = residual.shape[0] <= 4 * slots and lax.axis_size("tensor") == 4
     if spread_all:
         normed = normed_rows(attn_partial, residual, norm_gain)
+        payload = rotated_rows(normed, channel_order, rotation)
     else:
         summed = lax.psum_scatter(
             attn_partial[0].astype(jnp.float32).astype(jnp.bfloat16),
@@ -483,7 +527,7 @@
         hidden = residual.astype(jnp.float32) + summed
         scale = lax.rsqrt(jnp.mean(hidden * hidden, axis=1, keepdims=True) + 1e-06)
         normed = (hidden * scale * norm_gain[None, :]).astype(jnp.bfloat16)
-    payload = rotate_rows(normed, channel_order, rotation)
+        payload = rotate_rows(normed, channel_order, rotation)
     start = slab_block[0] * rotation.shape[1]
     if spread_all:
         return gathered_gram(payload, routes, slab_block, rotation.shape[1])[None]

time: 207 us -> 202 us (0.976)
  local copies, waits for them, and re-layouts: 38.1 us -> 8.26 us
  Pallas kernels: 163 us -> 190 us
    gather x2 -> x0, local copies, waits for them, and re-layouts: 27.8 us -> none  [rotate_rows(): moved = jnp.take(rows, channel_order, axis=1)]
    pallas_call x0 -> x1, Pallas kernels: none -> 26.5 us  [rotated_rows(): pl.pallas_call(rotated_kernel, out_shape=jax.ShapeDtypeStruct((local, wid...]
    unnamed x4 -> x2, local copies, waits for them, and re-layouts: 7.41 us -> 7.38 us
where the time goes in v5:
time: 202 us; the launch traced here: 201 us
  Pallas kernels  190 us (94%)
  local copies, waits for them, and re-layouts  8.26 us (4%)
  other arithmetic  2.36 us (1%)
    pallas_call x1, Pallas kernels, gathered_gram(): pl.pallas_call(functools.partial(gram_kernel, planes, local, width, colum...  135 us
    pallas_call x1, Pallas kernels, normed_rows(): pl.pallas_call(functools.partial(normed_kernel, local), out_shape=jax.Sha...  28.2 us
    pallas_call x1, Pallas kernels, rotated_rows(): pl.pallas_call(rotated_kernel, out_shape=jax.ShapeDtypeStruct((local, wid...  26.5 us
    unnamed x2, local copies, waits for them, and re-layouts  7.38 us

profile of v5, /device:TPU:0, one launch (start us, length us, event | category | flops | bytes accessed | tf_op | source)
XLA Modules:
  0.0 200.8 jit_solution(12785182325339069649)
XLA Ops:
  0.7 0.1 copy.12
  0.8 0.1 convert_element_type.6
  0.9 0.8 copy.13
  1.7 0.2 fusion
  1.8 0.7 broadcast_in_dim.6.bits_ref
  2.5 28.2 %normed_rows.1.rows_ref = bf16[64,7168]{1,0:T(8,128)(2,1)} custom-call(bf16[1,256,7168]{2,1,0:T(8,128)(2,1)} %partial_ref.1, bf16[64,7168]{1,0:T(8,128)(2,1)} %residual_ref.1, f32[1,7168]{1,0:T(1,128)} %bitcast.5), custom_call_target="tpu_custom_call" | custom-call | tf_op jit(solution)/shard_map/normed_rows/pallas_call | solution.py:444
  30.7 26.5 %rotated_rows.1 = bf16[64,7168]{1,0:T(8,128)(2,1)} custom-call(s32[7168]{0:T(1024)} %order_ref.1, bf16[64,7168]{1,0:T(8,128)(2,1)} %normed_rows.1.rows_ref, bf16[56,128,128]{2,1,0:T(8,128)(2,1)} %rotation_ref.1), custom_call_target="tpu_custom_call" | custom-call | tf_op jit(solution)/shard_map/rotated_rows/pallas_call | solution.py:495
  57.2 2.2 %pad_maximum_fusion.own_ref = bf16[64,7296]{1,0:T(8,128)(2,1)} fusion(bf16[64,128]{1,0:T(8,128)(2,1)S(1)} %convert_element_type.7, bf16[64,7168]{1,0:T(8,128)(2,1)} %rotated_rows.1), kind=kLoop, calls=%fused_computation | loop fusion | flops 1867776 | bytes 1867776 | tf_op jit(solution)/shard_map/concatenate | solution.py:321
  59.3 134.9 %gathered_gram.1 = bf16[7168,512]{1,0:T(8,128)(2,1)} custom-call(bf16[12,16,128]{2,1,0:T(8,128)(2,1)} %broadcast_in_dim.6.bits_ref, bf16[64,7296]{1,0:T(8,128)(2,1)} %pad_maximum_fusion.own_ref), custom_call_target="tpu_custom_call" | custom-call | tf_op jit(solution)/shard_map/gathered_gram/pallas_call | solution.py:330
  194.2 6.6 %copy.16 = bf16[1,7168,512]{2,1,0:T(8,128)(2,1)} copy(bf16[1,7168,512]{2,1,0:T(8,128)(2,1)} %bitcast.4) | data formatting | bytes 14680064
  (3 shorter events, 0.0 us)
